TPU v7x, 32 devices: a whole 2x2x4 slice. The times are simulated.
32 devices in a mesh: cuts: 2 (over x), frame: 8 (over z, y), coil: 2 (over core).
Axes of the slice: x: 2, y: 2, z: 4, core: 2. Of those that a mesh axis runs over, the one named last changes fastest.
Arguments:
- spatial: bfloat16 [512, 32, 512], P(('cuts', 'coil', 'frame')), parts along dimension 0, may hold values from -6 to 6
- temporal: bfloat16 [32, 64], P(('cuts', 'frame')), parts along dimension 0, may hold values from -0.75 to 0.75
- kspace: bfloat16 [32, 32, 256, 512], P(('cuts', 'frame'), 'coil'), parts along dimension 0, may hold values from -2 to 2
- sampled: int32 [32, 256], P(('cuts', 'frame')), parts along dimension 0, may hold values 0 or 1
- sensitivity: bfloat16 [64, 256, 512], P(('cuts', 'coil')), parts along dimension 0, may hold values from -1 to 1
Outputs:
- spatial_grad: float32 [512, 32, 512], P(('cuts', 'coil', 'frame')), parts along dimension 0
- temporal_grad: float32 [32, 64], P(('cuts', 'frame')), parts along dimension 0
There are 2 independent parts, one for each index of `cuts`. A program takes and returns all parts, laid end to end along the dimension named above; each array names one. Nothing has to cross between parts.
All inputs are finite; a program needn't handle non-finite values. No bound on the sum of `sampled` on one device may be relied on, other than what follows from the above.
Results may differ from a plain program's by a relative error of at most 0.003.
Values may be sent and summed in bfloat16 or wider, within the bound.
No kernel may reach another device: no remote copies, remote signals or barrier semaphores. Data moves between devices by JAX's collectives and lax.ppermute only.
A program may use at most 128 MiB of HBM per device.

v0:
```python
import math
import jax
import jax.numpy as jnp
from jax import lax
from jax.sharding import PartitionSpec as P


def split_parts(values):
    half_width = values.shape[-1] // 2
    return (values[..., :half_width], values[..., half_width:])


def dft_block(length):
    index = jnp.arange(length, dtype=jnp.int32)
    angles = (index[:, None] * index[None, :] % length).astype(jnp.float32) * (
        2.0 * math.pi / length
    )
    norm_factor = 1.0 / math.sqrt(length)
    cosine = jnp.cos(angles) * norm_factor
    sine_part = -jnp.sin(angles) * norm_factor
    upper_rows = jnp.concatenate([cosine, sine_part], 1)
    lower_rows = jnp.concatenate([-sine_part, cosine], 1)
    return jnp.concatenate([upper_rows, lower_rows], 0).astype(jnp.bfloat16)


def to_image(temporal, spatial):
    temp_real, temp_imag = split_parts(temporal)
    spat_real, spat_imag = split_parts(spatial)
    image_real = jnp.einsum(
        "tr,xry->txy", temp_real, spat_real, preferred_element_type=jnp.float32
    ) - jnp.einsum("tr,xry->txy", temp_imag, spat_imag, preferred_element_type=jnp.float32)
    image_imag = jnp.einsum(
        "tr,xry->txy", temp_real, spat_imag, preferred_element_type=jnp.float32
    ) + jnp.einsum("tr,xry->txy", temp_imag, spat_real, preferred_element_type=jnp.float32)
    return jnp.concatenate([image_real, image_imag], -1).astype(jnp.bfloat16)


def factor_grad(temporal, grad_image):
    temp_real, temp_imag = split_parts(temporal)
    grad_real, grad_imag = split_parts(grad_image)
    spatial_real = jnp.einsum(
        "tr,txy->xry", temp_real, grad_real, preferred_element_type=jnp.float32
    ) + jnp.einsum("tr,txy->xry", temp_imag, grad_imag, preferred_element_type=jnp.float32)
    spatial_imag = jnp.einsum(
        "tr,txy->xry", temp_real, grad_imag, preferred_element_type=jnp.float32
    ) - jnp.einsum("tr,txy->xry", temp_imag, grad_real, preferred_element_type=jnp.float32)
    return jnp.concatenate([spatial_real, spatial_imag], -1)


def frame_grad(spatial, grad_image):
    spat_real, spat_imag = split_parts(spatial)
    grad_real, grad_imag = split_parts(grad_image)
    temporal_real = jnp.einsum(
        "xry,txy->tr", spat_real, grad_real, preferred_element_type=jnp.float32
    ) + jnp.einsum("xry,txy->tr", spat_imag, grad_imag, preferred_element_type=jnp.float32)
    temporal_imag = jnp.einsum(
        "xry,txy->tr", spat_real, grad_imag, preferred_element_type=jnp.float32
    ) - jnp.einsum("xry,txy->tr", spat_imag, grad_real, preferred_element_type=jnp.float32)
    return jnp.concatenate([temporal_real, temporal_imag], -1)


def coil_adjoint(image, measured, sampled_row, sensitivity, block):
    image_real, image_imag = split_parts(image.astype(jnp.float32))
    sens_real, sens_imag = split_parts(sensitivity.astype(jnp.float32))
    coil_real = sens_real * image_real[None] - sens_imag * image_imag[None]
    coil_imag = sens_real * image_imag[None] + sens_imag * image_real[None]
    coil_image = jnp.concatenate([coil_real, coil_imag], -1).astype(jnp.bfloat16)
    coil_count, row_count, full_width = coil_image.shape
    spectrum = jnp.dot(
        coil_image.reshape(coil_count * row_count, full_width),
        block,
        preferred_element_type=jnp.float32,
    ).reshape(coil_count, row_count, full_width)
    line_keep = jnp.concatenate([sampled_row, sampled_row]).astype(jnp.float32)
    misfit = (line_keep * (spectrum - measured.astype(jnp.float32))).astype(jnp.bfloat16)
    adjoint = jnp.dot(
        misfit.reshape(coil_count * row_count, full_width),
        block.T,
        preferred_element_type=jnp.float32,
    ).reshape(coil_count, row_count, full_width)
    back_real, back_imag = split_parts(adjoint)
    grad_real = jnp.sum(sens_real * back_real + sens_imag * back_imag, axis=0)
    grad_imag = jnp.sum(sens_real * back_imag - sens_imag * back_real, axis=0)
    return jnp.concatenate([grad_real, grad_imag], -1)


def on_device(spatial, temporal, kspace, sampled, sensitivity):
    block = dft_block(spatial.shape[2] // 2)
    temporal_all = lax.all_gather(temporal, "frame", axis=0, tiled=True)
    image_rows = to_image(temporal_all, spatial)
    image_half = lax.all_to_all(image_rows, "frame", split_axis=0, concat_axis=1, tiled=True)
    image_full = lax.all_gather(image_half, "coil", axis=1, tiled=True)
    coil_partial = lax.map(
        lambda frame_item: coil_adjoint(
            frame_item[0], frame_item[1], frame_item[2], sensitivity, block
        ),
        (image_full, kspace, sampled),
    )
    grad_half = lax.psum_scatter(coil_partial, "coil", scatter_dimension=1, tiled=True).astype(
        jnp.bfloat16
    )
    grad_rows = lax.all_to_all(grad_half, "frame", split_axis=1, concat_axis=0, tiled=True)
    spatial_grad = factor_grad(temporal_all, grad_rows)
    temporal_part = lax.psum_scatter(
        frame_grad(spatial, grad_rows), "frame", scatter_dimension=0, tiled=True
    )
    temporal_grad = lax.psum(temporal_part, "coil")
    return (spatial_grad, temporal_grad)


def solution(mesh):
    placed = (
        P(("cuts", "coil", "frame"), None, None),
        P(("cuts", "frame"), None),
        P(("cuts", "frame"), "coil", None, None),
        P(("cuts", "frame"), None),
        P(("cuts", "coil"), None, None),
    )
    return jax.shard_map(
        on_device,
        mesh=mesh,
        in_specs=placed,
        out_specs=(P(("cuts", "coil", "frame"), None, None), P(("cuts", "frame"), None)),
        check_vma=False,
    )
```

profile of v0, /device:TPU:0, one launch (start us, length us, event | category | flops | bytes accessed | tf_op | source)
XLA Modules:
  0.0 152.4 jit_solution(3036720703098302424)
XLA Ops:
  0.6 22.5 %all-gather = bf16[8,2,64]{2,1,0:T(2,128)(2,1)S(1)} all-gather(bf16[1,2,64]{2,1,0:T(2,128)(2,1)} %bitcast.83), channel_id=1, replica_groups=mesh['cuts'=2,'frame'=8,'coil'=2] {'frame'}, dimensions={0}, use_global_device_ids=true | all-gather | bytes 2304 | tf_op jit(solution)/shard_map/all_gather | solution.py:89
  23.1 1.1 fusion.41
  24.2 1.1 fusion.35
  25.3 1.2 fusion.22
  26.5 1.2 fusion.23
  28.6 3.4 %all-to-all-start = ((bf16[16,16,512]{2,1,0:T(8,128)(2,1)}), bf16[16,16,512]{2,1,0:T(8,128)(2,1)S(1)}, u32[]{:S(2)}, u32[]{:S(2)}) async-start(bf16[16,16,512]{2,1,0:T(8,128)(2,1)} %copy.13), calls=%async_computation | async-start | bytes 524288 | tf_op jit(solution)/shard_map/all_to_all | solution.py:91
  32.0 1.3 dynamic-slice
  33.9 1.0 fusion.32
  34.9 1.1 negate_convert_fusion
  36.9 3.3 %all-to-all-done = bf16[16,16,512]{2,1,0:T(8,128)(2,1)S(1)} async-done(((bf16[16,16,512]{2,1,0:T(8,128)(2,1)}), bf16[16,16,512]{2,1,0:T(8,128)(2,1)S(1)}, u32[]{:S(2)}, u32[]{:S(2)}) %all-to-all-start) | async-done | bytes 262176 | tf_op jit(solution)/shard_map/all_to_all | solution.py:91
  40.2 2.2 %all_gather.7 = bf16[2,256,512]{2,1,0:T(8,128)(2,1)S(1)} all-gather(bf16[2,128,512]{2,1,0:T(8,128)(2,1)S(1)} %bitcast.70), channel_id=1, replica_groups=mesh['cuts'=2,'frame'=8,'coil'=2] {'coil'}, dimensions={1}, use_global_device_ids=true | all-gather | bytes 786432 | tf_op jit(solution)/shard_map/all_gather | solution.py:92
  42.4 62.9 %while.10 = (s32[]{:T(128)}, f32[2,256,512]{2,0,1:T(2,128)}, bf16[16,256,512]{2,1,0:T(8,128)(2,1)}, s32[2,256]{1,0:T(2,128)S(1)}, bf16[2,256,512]{2,1,0:T(8,128)...) while((s32[]{:T(128)}, f32[2,256,512]{2,0,1:T(2,128)}, ...), condition=%wide.region_3.4_spmd, body=%wide.region_0.3_spmd.sunk | while | flops 4330750976 | bytes 107749048 | solution.py:93
  42.5 3.4 %convert_element_type.64 = f32[16,256,512]{2,1,0:T(8,128)S(1)} convert(bf16[16,256,512]{2,1,0:T(8,128)(2,1)} %get-tuple-element.137) | non-fusion elementwise | flops 2097152 | bytes 12582912 | tf_op jit(solution)/shard_map/while/body/eval_jaxpr/convert_element_type | solution.py:64
  45.9 3.0 %subtract_convert_fusion.2 = (bf16[16,256,256]{2,1,0:T(8,128)(2,1)S(1)}, bf16[16,256,256]{2,1,0:T(8,128)(2,1)}) fusion(f32[16,256,512]{2,1,0:T(8,128)S(1)} %convert_element_type.64, f32[256,256]{1,0:T(8,128)S(1)} %get-tuple-element.111, f32[256,256]{1,0:T(8,128)S(1)} %get-tuple-element.112), kind=kLoop, calls=%fused_computation.13.clone.1 | loop fusion | flops 8388608 | bytes 13107200 | tf_op jit(solution)/shard_map/convert.2
  48.8 0.9 copy-done
  49.7 10.8 %fusion.65 = f32[16,256,512]{2,1,0:T(8,128)} fusion(bf16[2,16,256,512]{3,2,1,0:T(8,128)(2,1)} %get-tuple-element.141, s32[]{:T(128)} %get-tuple-element.126, f32[512]{0:T(512)S(1)} %add_convert_fusion.3, bf16[16,256,256]{2,1,0:T(8,128)(2,1)} %get-tuple-element.113, bf16[16,256,256]{2,1,0:T(8,128)(2,1)S(1)} %get-tuple-element.114, ...), kind=kOutput, calls=%fused_computation.3.clone.1 | convolution fusion | flops 4311744512 | bytes 17828352 | tf_op jit(solution)/shard_map/while/body/eval_jaxpr/dot_general | solution.py:76
  60.5 7.0 %add_reduce_fusion.2 = (f32[256,256]{1,0:T(8,128)S(1)}, f32[256,256]{1,0:T(8,128)S(1)}) fusion(f32[16,256,512]{2,1,0:T(8,128)} %fusion.65, f32[16,256,512]{2,1,0:T(8,128)} %copy-done), kind=kLoop, calls=%fused_computation.10.clone.1 | loop fusion | flops 8257536 | bytes 17301504 | tf_op jit(solution)/shard_map/while/body/eval_jaxpr/reduce_sum | solution.py:82
  68.2 4.7 %dynamic_update_slice.5 = f32[2,256,512]{2,0,1:T(2,128)S(1)} dynamic-update-slice(f32[2,256,512]{2,0,1:T(2,128)S(1)} %copy-done.2, f32[1,256,512]{2,0,1:T(1,128)S(1)} %copy.22, s32[]{:T(128)} %get-tuple-element.126, s32[]{:T(128)} %constant.31.clone.1..sunk, s32[]{:T(128)} %constant.31.clone.1..sunk) | dynamic-update-slice | bytes 1048580 | tf_op jit(solution)/shard_map/while/body/jit(dynamic_update_index_in_dim)/dynamic_update_slice | solution.py:93
  72.9 1.0 copy-done.3
  74.0 3.3 %convert_element_type.64 = f32[16,256,512]{2,1,0:T(8,128)S(1)} convert(bf16[16,256,512]{2,1,0:T(8,128)(2,1)} %get-tuple-element.137) | non-fusion elementwise | flops 2097152 | bytes 12582912 | tf_op jit(solution)/shard_map/while/body/eval_jaxpr/convert_element_type | solution.py:64
  77.3 3.0 %subtract_convert_fusion.2 = (bf16[16,256,256]{2,1,0:T(8,128)(2,1)S(1)}, bf16[16,256,256]{2,1,0:T(8,128)(2,1)}) fusion(f32[16,256,512]{2,1,0:T(8,128)S(1)} %convert_element_type.64, f32[256,256]{1,0:T(8,128)S(1)} %get-tuple-element.111, f32[256,256]{1,0:T(8,128)S(1)} %get-tuple-element.112), kind=kLoop, calls=%fused_computation.13.clone.1 | loop fusion | flops 8388608 | bytes 13107200 | tf_op jit(solution)/shard_map/convert.2
  81.2 10.8 %fusion.65 = f32[16,256,512]{2,1,0:T(8,128)} fusion(bf16[2,16,256,512]{3,2,1,0:T(8,128)(2,1)} %get-tuple-element.141, s32[]{:T(128)} %get-tuple-element.126, f32[512]{0:T(512)S(1)} %add_convert_fusion.3, bf16[16,256,256]{2,1,0:T(8,128)(2,1)} %get-tuple-element.113, bf16[16,256,256]{2,1,0:T(8,128)(2,1)S(1)} %get-tuple-element.114, ...), kind=kOutput, calls=%fused_computation.3.clone.1 | convolution fusion | flops 4311744512 | bytes 17828352 | tf_op jit(solution)/shard_map/while/body/eval_jaxpr/dot_general | solution.py:76
  91.9 7.0 %add_reduce_fusion.2 = (f32[256,256]{1,0:T(8,128)S(1)}, f32[256,256]{1,0:T(8,128)S(1)}) fusion(f32[16,256,512]{2,1,0:T(8,128)} %fusion.65, f32[16,256,512]{2,1,0:T(8,128)} %copy-done), kind=kLoop, calls=%fused_computation.10.clone.1 | loop fusion | flops 8257536 | bytes 17301504 | tf_op jit(solution)/shard_map/while/body/eval_jaxpr/reduce_sum | solution.py:82
  99.6 4.7 %dynamic_update_slice.5 = f32[2,256,512]{2,0,1:T(2,128)S(1)} dynamic-update-slice(f32[2,256,512]{2,0,1:T(2,128)S(1)} %copy-done.2, f32[1,256,512]{2,0,1:T(1,128)S(1)} %copy.22, s32[]{:T(128)} %get-tuple-element.126, s32[]{:T(128)} %constant.31.clone.1..sunk, s32[]{:T(128)} %constant.31.clone.1..sunk) | dynamic-update-slice | bytes 1048580 | tf_op jit(solution)/shard_map/while/body/jit(dynamic_update_index_in_dim)/dynamic_update_slice | solution.py:93
  104.3 1.0 copy-done.3
  105.3 6.9 %all-reduce.3 = bf16[2,256,512]{2,0,1:T(2,128)(2,1)S(1)} all-reduce(f32[2,256,512]{2,0,1:T(2,128)} %get-tuple-element.39), channel_id=2, replica_groups=mesh['cuts'=2,'frame'=8,'coil'=2] {'coil'}, use_global_device_ids=true, to_apply=%region_4.5.clone | all-reduce | flops 262144 | bytes 1572864
  112.2 0.9 dynamic-slice_convert_fusion
  113.1 3.4 %all-to-all-start.1 = ((bf16[2,128,512]{2,0,1:T(2,128)(2,1)}), bf16[2,128,512]{2,0,1:T(2,128)(2,1)S(1)}, u32[]{:S(2)}, u32[]{:S(2)}) async-start(bf16[2,128,512]{2,0,1:T(2,128)(2,1)} %dynamic-slice_convert_fusion), calls=%async_computation.1 | async-start | bytes 524288 | tf_op jit(solution)/shard_map/all_to_all | solution.py:102
  117.7 8.4 %all-to-all-done.1 = bf16[2,128,512]{2,0,1:T(2,128)(2,1)S(1)} async-done(((bf16[2,128,512]{2,0,1:T(2,128)(2,1)}), bf16[2,128,512]{2,0,1:T(2,128)(2,1)S(1)}, u32[]{:S(2)}, u32[]{:S(2)}) %all-to-all-start.1) | async-done | bytes 262176 | tf_op jit(solution)/shard_map/all_to_all | solution.py:102
  127.9 19.6 %all-reduce.1 = f32[16,64]{1,0:T(8,128)S(1)} all-reduce(f32[16,64]{1,0:T(8,128)S(1)} %pad_maximum_fusion.2), channel_id=3, replica_groups=mesh['cuts'=2,'frame'=8,'coil'=2] {'frame'}, use_global_device_ids=true, to_apply=%region_5.6.clone | all-reduce | flops 1024 | bytes 8192
  147.6 3.0 %psum.7 = f32[2,64]{1,0:T(2,128)} all-reduce(f32[2,64]{1,0:T(2,128)S(1)} %constant_dynamic-slice_fusion.1), channel_id=1, replica_groups=mesh['cuts'=2,'frame'=8,'coil'=2] {'coil'}, use_global_device_ids=true, to_apply=%region_6.7 | all-reduce | flops 128 | bytes 1024 | tf_op jit(solution)/shard_map/psum | solution.py:107
  151.3 1.1 pad_maximum_fusion
  (45 shorter events, 7.0 us)
Async XLA Ops:
  0.6 41.7 %copy-start.4 = (s32[2,256]{1,0:T(2,128)S(1)}, s32[2,256]{1,0:T(2,128)}, u32[]{:S(2)}) copy-start(s32[2,256]{1,0:T(2,128)} %param.10) | copy-start | bytes 6148
  28.6 11.6 %all-to-all-start = ((bf16[16,16,512]{2,1,0:T(8,128)(2,1)}), bf16[16,16,512]{2,1,0:T(8,128)(2,1)S(1)}, u32[]{:S(2)}, u32[]{:S(2)}) async-start(bf16[16,16,512]{2,1,0:T(8,128)(2,1)} %copy.13), calls=%async_computation | async-start | bytes 524288 | tf_op jit(solution)/shard_map/all_to_all | solution.py:91
  42.4 74.1 %copy-start.5 = (u32[32]{0:T(128)S(1)}, u32[32]{0:T(128)}, u32[]{:S(2)}) copy-start(u32[32]{0:T(128)} %constant.47) | copy-start | bytes 388
  42.4 84.1 %copy-start.1 = (bf16[16,32,512]{2,1,0:T(8,128)(2,1)S(1)}, bf16[16,32,512]{2,1,0:T(8,128)(2,1)}, u32[]{:S(2)}) copy-start(bf16[16,32,512]{2,1,0:T(8,128)(2,1)} %param.7) | copy-start | bytes 1572868
  45.9 3.8 %copy-start = (f32[16,256,512]{2,1,0:T(8,128)}, f32[16,256,512]{2,1,0:T(8,128)S(1)}, u32[]{:S(2)}) copy-start(f32[16,256,512]{2,1,0:T(8,128)S(1)} %convert_element_type.64) | copy-start | bytes 25165828 | tf_op jit(solution)/shard_map/while
  60.5 7.6 %copy-start.2 = (f32[2,256,512]{2,0,1:T(2,128)S(1)}, f32[2,256,512]{2,0,1:T(2,128)}, u32[]{:S(2)}) copy-start(f32[2,256,512]{2,0,1:T(2,128)} %get-tuple-element.127) | copy-start | bytes 3145732 | tf_op jit(solution)/shard_map/while
  72.9 1.0 copy-start.3
  77.3 3.8 %copy-start = (f32[16,256,512]{2,1,0:T(8,128)}, f32[16,256,512]{2,1,0:T(8,128)S(1)}, u32[]{:S(2)}) copy-start(f32[16,256,512]{2,1,0:T(8,128)S(1)} %convert_element_type.64) | copy-start | bytes 25165828 | tf_op jit(solution)/shard_map/while
  91.9 7.6 %copy-start.2 = (f32[2,256,512]{2,0,1:T(2,128)S(1)}, f32[2,256,512]{2,0,1:T(2,128)}, u32[]{:S(2)}) copy-start(f32[2,256,512]{2,0,1:T(2,128)} %get-tuple-element.127) | copy-start | bytes 3145732 | tf_op jit(solution)/shard_map/while
  104.3 1.0 copy-start.3
  113.1 13.1 %all-to-all-start.1 = ((bf16[2,128,512]{2,0,1:T(2,128)(2,1)}), bf16[2,128,512]{2,0,1:T(2,128)(2,1)S(1)}, u32[]{:S(2)}, u32[]{:S(2)}) async-start(bf16[2,128,512]{2,0,1:T(2,128)(2,1)} %dynamic-slice_convert_fusion), calls=%async_computation.1 | async-start | bytes 524288 | tf_op jit(solution)/shard_map/all_to_all | solution.py:102
where the time goes:
time: 153 us; the launch traced here: 152 us
  blocking collectives  54.2 us (35%)
  other arithmetic  31 us (20%)
  matrix products  28.1 us (18%)
  local copies, waits for them, and re-layouts  18.2 us (12%)
  waiting for transfers between devices  11.7 us (8%)
  starting transfers between devices  6.82 us (4%)
  between operations  2.1 us (1%)
    unnamed x2, blocking collectives  26.5 us
    all_gather x1, blocking collectives, on_device(): temporal_all = lax.all_gather(temporal, 'frame', axis=0, tiled=True)  22.5 us
    dot_general x2, matrix products, coil_adjoint(): jnp.dot(misfit.reshape(coil_count * row_count, full_width), block.T, pref...  21.6 us
    reduce_sum x2, other arithmetic, coil_adjoint(): grad_real = jnp.sum(sens_real * back_real + sens_imag * back_imag, axis=0)  14 us
    dynamic_update_slice x4, local copies, waits for them, and re-layouts, on_device(): lax.map(lambda frame_item: coil_adjoint(frame_item[0], frame_item[1], fra...  10.5 us
    all_to_all x1, waiting for transfers between devices, on_device(): lax.all_to_all(grad_half, 'frame', split_axis=1, concat_axis=0, tiled=True)  8.41 us
    another operation x4, other arithmetic  8 us
    convert_element_type x2, other arithmetic, coil_adjoint(): sens_real, sens_imag = split_parts(sensitivity.astype(jnp.float32))  6.72 us
  transfers between devices with their start and end apart: 2, of which 2 were waited for; matrix products, arithmetic and copies ran while one was open for 3% of the time, Pallas kernels for 0%

commit v1 on v0

--- a/solution.py
+++ b/solution.py
@@ -3,6 +3,29 @@
 import jax.numpy as jnp
 from jax import lax
 from jax.sharding import PartitionSpec as P
+
+
+def in_order(tiles, dim):
+    lengths = list(tiles.shape[1:])
+    lengths[dim] *= tiles.shape[0]
+    return jnp.moveaxis(tiles, 0, dim).reshape(lengths)
+
+
+def collected_by_bits(x, axis):
+    size, index = (lax.axis_size(axis), lax.axis_index(axis))
+    parts, distance = (x[None], 1)
+    while distance < size:
+        partner_block = lax.ppermute(parts, axis, [(i, i ^ distance) for i in range(size)])
+        low = index & distance == 0
+        parts = jnp.concatenate(
+            [jnp.where(low, parts, partner_block), jnp.where(low, partner_block, parts)]
+        )
+        distance *= 2
+    return parts
+
+
+def gather_by_bits(x, axis, dim):
+    return in_order(collected_by_bits(x, axis), dim)
 
 
 def split_parts(values):
@@ -86,7 +109,7 @@
 
 def on_device(spatial, temporal, kspace, sampled, sensitivity):
     block = dft_block(spatial.shape[2] // 2)
-    temporal_all = lax.all_gather(temporal, "frame", axis=0, tiled=True)
+    temporal_all = gather_by_bits(temporal, "frame", 0)
     image_rows = to_image(temporal_all, spatial)
     image_half = lax.all_to_all(image_rows, "frame", split_axis=0, concat_axis=1, tiled=True)
     image_full = lax.all_gather(image_half, "coil", axis=1, tiled=True)

time: 153 us -> 147 us (0.961)
  blocking collectives: 54.2 us -> 31.7 us
  starting transfers between devices: 6.82 us -> 17.9 us
  waiting for transfers between devices: 11.7 us -> 16.6 us
    all_gather x1 -> x0, blocking collectives: 22.5 us -> none  [on_device(): temporal_all = lax.all_gather(temporal, 'frame', axis=0, tiled=True)]
    ppermute x0 -> x3, starting transfers between devices: none -> 8.3 us  [collected_by_bits(): lax.ppermute(parts, axis, [(i, i ^ distance) for i in range(size)])]
    ppermute x0 -> x3, waiting for transfers between devices: none -> 4.8 us  [collected_by_bits(): lax.ppermute(parts, axis, [(i, i ^ distance) for i in range(size)])]
    all_to_all x1, starting transfers between devices: 3.41 us -> 6.16 us  [on_device(): lax.all_to_all(image_rows, 'frame', split_axis=0, concat_axis=1, tiled=True)]
  transfers between devices with their start and end apart: 2 -> 5, of which waited for: 2 -> 5; matrix products, arithmetic and copies ran while one was open for 3% -> 3% of each run, Pallas kernels for 0% -> 0%
where the time goes in v1:
time: 147 us
  other arithmetic  31.7 us (22%)
  blocking collectives  31.7 us (22%)
  matrix products  28.1 us (19%)
  local copies, waits for them, and re-layouts  18.3 us (12%)
  starting transfers between devices  17.9 us (12%)
  waiting for transfers between devices  16.6 us (11%)
  between operations  2.1 us (1%)
    unnamed x2, blocking collectives  26.5 us
    dot_general x2, matrix products, coil_adjoint(): jnp.dot(misfit.reshape(coil_count * row_count, full_width), block.T, pref...  21.6 us
    reduce_sum x2, other arithmetic, coil_adjoint(): grad_real = jnp.sum(sens_real * back_real + sens_imag * back_imag, axis=0)  14 us
    dynamic_update_slice x4, local copies, waits for them, and re-layouts, on_device(): lax.map(lambda frame_item: coil_adjoint(frame_item[0], frame_item[1], fra...  10.5 us
    all_to_all x1, waiting for transfers between devices, on_device(): lax.all_to_all(grad_half, 'frame', split_axis=1, concat_axis=0, tiled=True)  8.41 us
    ppermute x3, starting transfers between devices, collected_by_bits(): lax.ppermute(parts, axis, [(i, i ^ distance) for i in range(size)])  8.3 us
    another operation x4, other arithmetic  7.99 us
    convert_element_type x2, other arithmetic, coil_adjoint(): sens_real, sens_imag = split_parts(sensitivity.astype(jnp.float32))  6.72 us
  transfers between devices with their start and end apart: 5, of which 5 were waited for; matrix products, arithmetic and copies ran while one was open for 3% of the time, Pallas kernels for 0%

profile of v1, /device:TPU:0, one launch (start us, length us, event | category | flops | bytes accessed | tf_op | source)
XLA Modules:
  0.0 146.6 jit_solution(997852255398467686)
XLA Ops:
  0.6 3.1 %collective-permute-start = (bf16[1,2,64]{2,1,0:T(2,128)(2,1)}, bf16[1,2,64]{2,1,0:T(2,128)(2,1)S(1)}, u32[]{:S(2)}, u32[]{:S(2)}) collective-permute-start(bf16[1,2,64]{2,1,0:T(2,128)(2,1)} %bitcast.85), channel_id=1, source_target_pairs={{0,2},{2,0},{4,6},{6,4},{8,10},{10,8},{12,14},{14,12},{1,3},{3,1},... | collective-permute-start | bytes 776 | tf_op jit(solution)/shard_map/ppermute | solution.py:18
  3.7 1.7 %collective-permute-done = bf16[1,2,64]{2,1,0:T(2,128)(2,1)S(1)} collective-permute-done((bf16[1,2,64]{2,1,0:T(2,128)(2,1)}, bf16[1,2,64]{2,1,0:T(2,128)(2,1)S(1)}, u32[]{:S(2)}, u32[]{:S(2)}) %collective-permute-start) | collective-permute-done | bytes 288 | tf_op jit(solution)/shard_map/ppermute | solution.py:18
  6.1 2.1 %collective-permute-start.1 = (bf16[2,2,64]{2,1,0:T(2,128)(2,1)S(1)}, bf16[2,2,64]{2,1,0:T(2,128)(2,1)S(1)}, u32[]{:S(2)}, u32[]{:S(2)}) collective-permute-start(bf16[2,2,64]{2,1,0:T(2,128)(2,1)S(1)} %pad_maximum_fusion.5), channel_id=1, source_target_pairs={{0,4},{2,6},{4,0},{6,2},{8,12},{10,14},{12,8},{14,10},{1,5},{3,7},... | collective-permute-start | bytes 1544 | tf_op jit(solution)/shard_map/ppermute | solution.py:18
  8.2 1.6 %collective-permute-done.1 = bf16[2,2,64]{2,1,0:T(2,128)(2,1)S(1)} collective-permute-done((bf16[2,2,64]{2,1,0:T(2,128)(2,1)S(1)}, bf16[2,2,64]{2,1,0:T(2,128)(2,1)S(1)}, u32[]{:S(2)}, u32[]{:S(2)}) %collective-permute-start.1) | collective-permute-done | bytes 544 | tf_op jit(solution)/shard_map/ppermute | solution.py:18
  9.8 3.1 %collective-permute-start.2 = (bf16[4,2,64]{2,1,0:T(2,128)(2,1)S(1)}, bf16[4,2,64]{2,1,0:T(2,128)(2,1)S(1)}, u32[]{:S(2)}, u32[]{:S(2)}) collective-permute-start(bf16[4,2,64]{2,1,0:T(2,128)(2,1)S(1)} %pad_maximum_fusion.4), channel_id=1, source_target_pairs={{0,8},{2,10},{4,12},{6,14},{8,0},{10,2},{12,4},{14,6},{1,9},{3,11}... | collective-permute-start | bytes 3080 | tf_op jit(solution)/shard_map/ppermute | solution.py:18
  12.9 1.6 %collective-permute-done.2 = bf16[4,2,64]{2,1,0:T(2,128)(2,1)S(1)} collective-permute-done((bf16[4,2,64]{2,1,0:T(2,128)(2,1)S(1)}, bf16[4,2,64]{2,1,0:T(2,128)(2,1)S(1)}, u32[]{:S(2)}, u32[]{:S(2)}) %collective-permute-start.2) | collective-permute-done | bytes 1056 | tf_op jit(solution)/shard_map/ppermute | solution.py:18
  14.5 1.1 fusion.41
  15.6 1.1 fusion.35
  16.7 1.2 fusion.22
  17.9 1.2 fusion.23
  20.0 6.2 %all-to-all-start = ((bf16[16,16,512]{2,1,0:T(8,128)(2,1)}), bf16[16,16,512]{2,1,0:T(8,128)(2,1)S(1)}, u32[]{:S(2)}, u32[]{:S(2)}) async-start(bf16[16,16,512]{2,1,0:T(8,128)(2,1)} %copy.13), calls=%async_computation | async-start | bytes 524288 | tf_op jit(solution)/shard_map/all_to_all | solution.py:114
  26.1 1.3 dynamic-slice
  29.0 1.1 negate_convert_fusion
  31.0 3.4 %all-to-all-done = bf16[16,16,512]{2,1,0:T(8,128)(2,1)S(1)} async-done(((bf16[16,16,512]{2,1,0:T(8,128)(2,1)}), bf16[16,16,512]{2,1,0:T(8,128)(2,1)S(1)}, u32[]{:S(2)}, u32[]{:S(2)}) %all-to-all-start) | async-done | bytes 262176 | tf_op jit(solution)/shard_map/all_to_all | solution.py:114
  34.4 2.2 %all_gather.3 = bf16[2,256,512]{2,1,0:T(8,128)(2,1)S(1)} all-gather(bf16[2,128,512]{2,1,0:T(8,128)(2,1)S(1)} %bitcast.72), channel_id=1, replica_groups=mesh['cuts'=2,'frame'=8,'coil'=2] {'coil'}, dimensions={1}, use_global_device_ids=true | all-gather | bytes 786432 | tf_op jit(solution)/shard_map/all_gather | solution.py:115
  36.6 63.0 %while.10 = (s32[]{:T(128)}, f32[2,256,512]{2,0,1:T(2,128)}, bf16[16,256,512]{2,1,0:T(8,128)(2,1)}, s32[2,256]{1,0:T(2,128)S(1)}, bf16[2,256,512]{2,1,0:T(8,128)...) while((s32[]{:T(128)}, f32[2,256,512]{2,0,1:T(2,128)}, ...), condition=%wide.region_3.4_spmd, body=%wide.region_0.3_spmd.sunk | while | flops 4330750976 | bytes 107749048 | solution.py:116
  36.7 3.4 %convert_element_type.64 = f32[16,256,512]{2,1,0:T(8,128)S(1)} convert(bf16[16,256,512]{2,1,0:T(8,128)(2,1)} %get-tuple-element.143) | non-fusion elementwise | flops 2097152 | bytes 12582912 | tf_op jit(solution)/shard_map/while/body/eval_jaxpr/convert_element_type | solution.py:87
  40.1 2.9 %subtract_convert_fusion.2 = (bf16[16,256,256]{2,1,0:T(8,128)(2,1)S(1)}, bf16[16,256,256]{2,1,0:T(8,128)(2,1)}) fusion(f32[16,256,512]{2,1,0:T(8,128)S(1)} %convert_element_type.64, f32[256,256]{1,0:T(8,128)S(1)} %get-tuple-element.117, f32[256,256]{1,0:T(8,128)S(1)} %get-tuple-element.118), kind=kLoop, calls=%fused_computation.13.clone.1 | loop fusion | flops 8388608 | bytes 13107200 | tf_op jit(solution)/shard_map/convert.2
  43.9 10.8 %fusion.65 = f32[16,256,512]{2,1,0:T(8,128)} fusion(bf16[2,16,256,512]{3,2,1,0:T(8,128)(2,1)} %get-tuple-element.147, s32[]{:T(128)} %get-tuple-element.132, f32[512]{0:T(512)S(1)} %add_convert_fusion.3, bf16[16,256,256]{2,1,0:T(8,128)(2,1)} %get-tuple-element.119, bf16[16,256,256]{2,1,0:T(8,128)(2,1)S(1)} %get-tuple-element.120, ...), kind=kOutput, calls=%fused_computation.3.clone.1 | convolution fusion | flops 4311744512 | bytes 17828352 | tf_op jit(solution)/shard_map/while/body/eval_jaxpr/dot_general | solution.py:99
  54.8 7.0 %add_reduce_fusion.2 = (f32[256,256]{1,0:T(8,128)S(1)}, f32[256,256]{1,0:T(8,128)S(1)}) fusion(f32[16,256,512]{2,1,0:T(8,128)} %fusion.65, f32[16,256,512]{2,1,0:T(8,128)} %copy-done), kind=kLoop, calls=%fused_computation.10.clone.1 | loop fusion | flops 8257536 | bytes 17301504 | tf_op jit(solution)/shard_map/while/body/eval_jaxpr/reduce_sum | solution.py:105
  62.4 4.7 %dynamic_update_slice.5 = f32[2,256,512]{2,0,1:T(2,128)S(1)} dynamic-update-slice(f32[2,256,512]{2,0,1:T(2,128)S(1)} %copy-done.2, f32[1,256,512]{2,0,1:T(1,128)S(1)} %copy.22, s32[]{:T(128)} %get-tuple-element.132, s32[]{:T(128)} %constant.24.clone.1..sunk, s32[]{:T(128)} %constant.24.clone.1..sunk) | dynamic-update-slice | bytes 1048580 | tf_op jit(solution)/shard_map/while/body/jit(dynamic_update_index_in_dim)/dynamic_update_slice | solution.py:116
  68.2 3.3 %convert_element_type.64 = f32[16,256,512]{2,1,0:T(8,128)S(1)} convert(bf16[16,256,512]{2,1,0:T(8,128)(2,1)} %get-tuple-element.143) | non-fusion elementwise | flops 2097152 | bytes 12582912 | tf_op jit(solution)/shard_map/while/body/eval_jaxpr/convert_element_type | solution.py:87
  71.5 2.9 %subtract_convert_fusion.2 = (bf16[16,256,256]{2,1,0:T(8,128)(2,1)S(1)}, bf16[16,256,256]{2,1,0:T(8,128)(2,1)}) fusion(f32[16,256,512]{2,1,0:T(8,128)S(1)} %convert_element_type.64, f32[256,256]{1,0:T(8,128)S(1)} %get-tuple-element.117, f32[256,256]{1,0:T(8,128)S(1)} %get-tuple-element.118), kind=kLoop, calls=%fused_computation.13.clone.1 | loop fusion | flops 8388608 | bytes 13107200 | tf_op jit(solution)/shard_map/convert.2
  75.4 10.8 %fusion.65 = f32[16,256,512]{2,1,0:T(8,128)} fusion(bf16[2,16,256,512]{3,2,1,0:T(8,128)(2,1)} %get-tuple-element.147, s32[]{:T(128)} %get-tuple-element.132, f32[512]{0:T(512)S(1)} %add_convert_fusion.3, bf16[16,256,256]{2,1,0:T(8,128)(2,1)} %get-tuple-element.119, bf16[16,256,256]{2,1,0:T(8,128)(2,1)S(1)} %get-tuple-element.120, ...), kind=kOutput, calls=%fused_computation.3.clone.1 | convolution fusion | flops 4311744512 | bytes 17828352 | tf_op jit(solution)/shard_map/while/body/eval_jaxpr/dot_general | solution.py:99
  86.2 7.0 %add_reduce_fusion.2 = (f32[256,256]{1,0:T(8,128)S(1)}, f32[256,256]{1,0:T(8,128)S(1)}) fusion(f32[16,256,512]{2,1,0:T(8,128)} %fusion.65, f32[16,256,512]{2,1,0:T(8,128)} %copy-done), kind=kLoop, calls=%fused_computation.10.clone.1 | loop fusion | flops 8257536 | bytes 17301504 | tf_op jit(solution)/shard_map/while/body/eval_jaxpr/reduce_sum | solution.py:105
  93.8 4.7 %dynamic_update_slice.5 = f32[2,256,512]{2,0,1:T(2,128)S(1)} dynamic-update-slice(f32[2,256,512]{2,0,1:T(2,128)S(1)} %copy-done.2, f32[1,256,512]{2,0,1:T(1,128)S(1)} %copy.22, s32[]{:T(128)} %get-tuple-element.132, s32[]{:T(128)} %constant.24.clone.1..sunk, s32[]{:T(128)} %constant.24.clone.1..sunk) | dynamic-update-slice | bytes 1048580 | tf_op jit(solution)/shard_map/while/body/jit(dynamic_update_index_in_dim)/dynamic_update_slice | solution.py:116
  99.5 6.9 %all-reduce.3 = bf16[2,256,512]{2,0,1:T(2,128)(2,1)S(1)} all-reduce(f32[2,256,512]{2,0,1:T(2,128)} %get-tuple-element.39), channel_id=2, replica_groups=mesh['cuts'=2,'frame'=8,'coil'=2] {'coil'}, use_global_device_ids=true, to_apply=%region_4.5.clone | all-reduce | flops 262144 | bytes 1572864
  107.3 3.4 %all-to-all-start.1 = ((bf16[2,128,512]{2,0,1:T(2,128)(2,1)}), bf16[2,128,512]{2,0,1:T(2,128)(2,1)S(1)}, u32[]{:S(2)}, u32[]{:S(2)}) async-start(bf16[2,128,512]{2,0,1:T(2,128)(2,1)} %dynamic-slice_convert_fusion), calls=%async_computation.1 | async-start | bytes 524288 | tf_op jit(solution)/shard_map/all_to_all | solution.py:125
  112.0 8.4 %all-to-all-done.1 = bf16[2,128,512]{2,0,1:T(2,128)(2,1)S(1)} async-done(((bf16[2,128,512]{2,0,1:T(2,128)(2,1)}), bf16[2,128,512]{2,0,1:T(2,128)(2,1)S(1)}, u32[]{:S(2)}, u32[]{:S(2)}) %all-to-all-start.1) | async-done | bytes 262176 | tf_op jit(solution)/shard_map/all_to_all | solution.py:125
  122.1 19.6 %all-reduce.1 = f32[16,64]{1,0:T(8,128)S(1)} all-reduce(f32[16,64]{1,0:T(8,128)S(1)} %pad_maximum_fusion.2), channel_id=3, replica_groups=mesh['cuts'=2,'frame'=8,'coil'=2] {'frame'}, use_global_device_ids=true, to_apply=%region_5.6.clone | all-reduce | flops 1024 | bytes 8192
  141.8 3.0 %psum.7 = f32[2,64]{1,0:T(2,128)} all-reduce(f32[2,64]{1,0:T(2,128)S(1)} %constant_dynamic-slice_fusion.1), channel_id=1, replica_groups=mesh['cuts'=2,'frame'=8,'coil'=2] {'coil'}, use_global_device_ids=true, to_apply=%region_6.7 | all-reduce | flops 128 | bytes 1024 | tf_op jit(solution)/shard_map/psum | solution.py:130
  145.5 1.1 pad_maximum_fusion
  (56 shorter events, 12.4 us)
Async XLA Ops:
  0.6 35.9 %copy-start.4 = (s32[2,256]{1,0:T(2,128)S(1)}, s32[2,256]{1,0:T(2,128)}, u32[]{:S(2)}) copy-start(s32[2,256]{1,0:T(2,128)} %param.10) | copy-start | bytes 6148
  0.6 4.7 %collective-permute-start = (bf16[1,2,64]{2,1,0:T(2,128)(2,1)}, bf16[1,2,64]{2,1,0:T(2,128)(2,1)S(1)}, u32[]{:S(2)}, u32[]{:S(2)}) collective-permute-start(bf16[1,2,64]{2,1,0:T(2,128)(2,1)} %bitcast.85), channel_id=1, source_target_pairs={{0,2},{2,0},{4,6},{6,4},{8,10},{10,8},{12,14},{14,12},{1,3},{3,1},... | collective-permute-start | bytes 776 | tf_op jit(solution)/shard_map/ppermute | solution.py:18
  6.1 3.7 %collective-permute-start.1 = (bf16[2,2,64]{2,1,0:T(2,128)(2,1)S(1)}, bf16[2,2,64]{2,1,0:T(2,128)(2,1)S(1)}, u32[]{:S(2)}, u32[]{:S(2)}) collective-permute-start(bf16[2,2,64]{2,1,0:T(2,128)(2,1)S(1)} %pad_maximum_fusion.5), channel_id=1, source_target_pairs={{0,4},{2,6},{4,0},{6,2},{8,12},{10,14},{12,8},{14,10},{1,5},{3,7},... | collective-permute-start | bytes 1544 | tf_op jit(solution)/shard_map/ppermute | solution.py:18
  9.8 4.7 %collective-permute-start.2 = (bf16[4,2,64]{2,1,0:T(2,128)(2,1)S(1)}, bf16[4,2,64]{2,1,0:T(2,128)(2,1)S(1)}, u32[]{:S(2)}, u32[]{:S(2)}) collective-permute-start(bf16[4,2,64]{2,1,0:T(2,128)(2,1)S(1)} %pad_maximum_fusion.4), channel_id=1, source_target_pairs={{0,8},{2,10},{4,12},{6,14},{8,0},{10,2},{12,4},{14,6},{1,9},{3,11}... | collective-permute-start | bytes 3080 | tf_op jit(solution)/shard_map/ppermute | solution.py:18
  20.0 14.4 %all-to-all-start = ((bf16[16,16,512]{2,1,0:T(8,128)(2,1)}), bf16[16,16,512]{2,1,0:T(8,128)(2,1)S(1)}, u32[]{:S(2)}, u32[]{:S(2)}) async-start(bf16[16,16,512]{2,1,0:T(8,128)(2,1)} %copy.13), calls=%async_computation | async-start | bytes 524288 | tf_op jit(solution)/shard_map/all_to_all | solution.py:114
  36.6 74.2 %copy-start.5 = (u32[32]{0:T(128)S(1)}, u32[32]{0:T(128)}, u32[]{:S(2)}) copy-start(u32[32]{0:T(128)} %constant.59) | copy-start | bytes 388
  36.6 84.2 %copy-start.1 = (bf16[16,32,512]{2,1,0:T(8,128)(2,1)S(1)}, bf16[16,32,512]{2,1,0:T(8,128)(2,1)}, u32[]{:S(2)}) copy-start(bf16[16,32,512]{2,1,0:T(8,128)(2,1)} %param.7) | copy-start | bytes 1572868
  40.1 3.9 %copy-start = (f32[16,256,512]{2,1,0:T(8,128)}, f32[16,256,512]{2,1,0:T(8,128)S(1)}, u32[]{:S(2)}) copy-start(f32[16,256,512]{2,1,0:T(8,128)S(1)} %convert_element_type.64) | copy-start | bytes 25165828 | tf_op jit(solution)/shard_map/while
  54.8 7.6 %copy-start.2 = (f32[2,256,512]{2,0,1:T(2,128)S(1)}, f32[2,256,512]{2,0,1:T(2,128)}, u32[]{:S(2)}) copy-start(f32[2,256,512]{2,0,1:T(2,128)} %get-tuple-element.133) | copy-start | bytes 3145732 | tf_op jit(solution)/shard_map/while
  67.1 1.0 copy-start.3
  71.5 3.9 %copy-start = (f32[16,256,512]{2,1,0:T(8,128)}, f32[16,256,512]{2,1,0:T(8,128)S(1)}, u32[]{:S(2)}) copy-start(f32[16,256,512]{2,1,0:T(8,128)S(1)} %convert_element_type.64) | copy-start | bytes 25165828 | tf_op jit(solution)/shard_map/while
  86.2 7.6 %copy-start.2 = (f32[2,256,512]{2,0,1:T(2,128)S(1)}, f32[2,256,512]{2,0,1:T(2,128)}, u32[]{:S(2)}) copy-start(f32[2,256,512]{2,0,1:T(2,128)} %get-tuple-element.133) | copy-start | bytes 3145732 | tf_op jit(solution)/shard_map/while
  98.6 1.0 copy-start.3
  107.3 13.1 %all-to-all-start.1 = ((bf16[2,128,512]{2,0,1:T(2,128)(2,1)}), bf16[2,128,512]{2,0,1:T(2,128)(2,1)S(1)}, u32[]{:S(2)}, u32[]{:S(2)}) async-start(bf16[2,128,512]{2,0,1:T(2,128)(2,1)} %dynamic-slice_convert_fusion), calls=%async_computation.1 | async-start | bytes 524288 | tf_op jit(solution)/shard_map/all_to_all | solution.py:125
